TPU v7x, 32 devices: a whole 2x2x4 slice. The times are simulated.
32 devices in a mesh: pair: 8 (over y, x, core), row: 4 (over z).
Axes of the slice: x: 2, y: 2, z: 4, core: 2. Of those that a mesh axis runs over, the one named last changes fastest.
Arguments:
- amplitudes: bfloat16 [3, 160, 32, 5120], P(None, 'pair', 'row'), may hold values from -6 to 6
- integrals: bfloat16 [3, 5120, 5120], P(None, 'row', 'pair'), may hold values from -0.078125 to 0.078125
- occupied_irrep: int32 [32], replicated, may hold values from 0 to 7
- virtual_order: int32 [1280], replicated, may hold values from 0 to 1279, each once
- block_irreps: int32 [3], replicated, may hold values from 0 to 7
- occupied_energy: float32 [32], replicated, may hold values from -2 to -0.5
- virtual_energy: float32 [1280], replicated, may hold values from 1 to 4
Outputs:
- update: float32 [3, 160, 32, 5120], P(None, None, 'row', 'pair')
Inputs may be any that keep to these rules, and one draw needn't show every extreme that they name: virtual_order holds every virtual orbital once; entries g * 160 to g * 160 + 159 are the virtual orbitals of irrep g.
All inputs are finite; a program needn't handle non-finite values.
Results may differ from a plain program's by a relative error of at most 0.0003.
Values may be sent and summed in bfloat16 or wider, within the bound.
A program may use at most 128 MiB of HBM per device.

v0:
```python
import jax
import jax.numpy as jnp
from jax import lax
from jax.sharding import PartitionSpec as P

VIRG = 160


def shift_table(occupied_irrep, virtual_order, block_irreps, occupied_energy, virtual_energy):
    count_virt = virtual_energy.shape[0]
    orbital_ids = jnp.arange(count_virt, dtype=jnp.int32)
    matches = virtual_order[:, None] == orbital_ids[None, :]
    slot_energy = jnp.sum(jnp.where(matches, virtual_energy[None, :], jnp.float32(0.0)), axis=1)
    irrep_count = count_virt // VIRG
    energy_grid = slot_energy.reshape(irrep_count, VIRG)
    pair_irrep = jnp.bitwise_xor(block_irreps[:, None], occupied_irrep[None, :])
    irrep_ids = jnp.arange(irrep_count, dtype=jnp.int32)
    chosen = pair_irrep[:, None, None, :] == irrep_ids[None, :, None, None]
    picked = jnp.sum(jnp.where(chosen, energy_grid[None, :, :, None], jnp.float32(0.0)), axis=1)
    return picked - occupied_energy[None, None, :]


def body(
    amplitudes,
    integrals,
    occupied_irrep,
    virtual_order,
    block_irreps,
    occupied_energy,
    virtual_energy,
):
    block_count, virt_local, occ_local, pair_width = amplitudes.shape
    column_width = integrals.shape[2]
    shift = shift_table(
        occupied_irrep, virtual_order, block_irreps, occupied_energy, virtual_energy
    )
    occ_start = lax.axis_index("row") * occ_local
    col_start = lax.axis_index("pair") * column_width
    results = []
    for block in range(block_count):
        whole_rows = lax.all_gather(integrals[block], "row", axis=0, tiled=True)
        piece = lax.all_gather(amplitudes[block], "pair", axis=0, tiled=True)
        flat = piece.reshape(piece.shape[0] * piece.shape[1], piece.shape[2])
        product = jnp.dot(flat, whole_rows, preferred_element_type=jnp.float32)
        cycle_term = product.reshape(piece.shape[0], piece.shape[1], whole_rows.shape[1])
        row_shift = lax.dynamic_slice_in_dim(shift[block], occ_start, occ_local, 1)
        col_shift = lax.dynamic_slice_in_dim(
            shift[block].reshape(pair_width), col_start, column_width, 0
        )
        denominator = row_shift[:, :, None] + col_shift[None, None, :]
        results.append(cycle_term / denominator)
    return jnp.stack(results)


def solution(mesh):
    placed = (P(None, "pair", "row", None), P(None, "row", "pair"), P(), P(), P(), P(), P())
    return jax.shard_map(
        body, mesh=mesh, in_specs=placed, out_specs=P(None, None, "row", "pair"), check_vma=False
    )
```

profile of v0, /device:TPU:0, one launch (start us, length us, event | category | flops | bytes accessed | tf_op | source)
XLA Modules:
  0.0 626.3 jit_solution(1180767231952461776)
XLA Ops:
  6.5 0.0 all-gather.19.cloned.1.call-start
  6.5 4.8 fusion.21
  11.4 0.0 all-gather.19.cloned.1.call-update
  11.4 0.0 all-gather.17.cloned.1.call-start
  11.5 4.7 slice_bitcast_fusion.2
  16.2 0.0 copy-start.3
  16.2 0.0 all-gather.17.cloned.1.call-update
  16.2 0.0 all-gather.15.cloned.1.call-start
  16.3 0.7 all-gather.15.cloned.1.call-update
  17.0 0.0 all-gather.13.cloned.1.call-start
  17.0 0.5 all-gather.13.cloned.1.call-update
  17.5 0.0 all-gather.23.cloned.1.call-start
  17.6 0.5 all-gather.23.cloned.1.call-update
  18.1 0.0 all-gather.21.cloned.1.call-start
  18.2 0.5 all-gather.21.cloned.1.call-update
  18.7 0.0 copy-done.1
  18.7 0.0 copy-done.2
  18.7 1.0 select_reduce_fusion
  19.7 0.1 broadcast_in_dim.51
  19.8 0.0 copy-done.4
  19.8 0.0 copy-done.5
  19.8 0.1 broadcast_xor_fusion
  19.9 0.2 select_reduce_fusion.1
  20.0 0.0 copy-done.3
  20.0 0.1 broadcast_subtract_fusion
  20.1 0.1 copy.22
  20.2 0.1 reshape_squeeze.10
  20.3 0.1 copy.21
  20.4 0.1 copy.19
  20.6 0.1 reshape_squeeze.9
  20.6 0.1 dynamic_slice.21
  20.7 0.1 dynamic_slice.19
  20.8 0.1 copy.18
  20.9 0.1 copy.25
  21.0 0.1 reshape_squeeze.11
  21.1 0.1 dynamic_slice.23
  21.2 0.1 copy.24
  21.3 112.6 %all-gather.19.cloned.1.call-done = bf16[1,5120,640]{2,1,0:T(8,128)(2,1)} async-done(((bf16[1,1280,640]{2,1,0:T(8,128)(2,1)}), bf16[1,5120,640]{2,1,0:T(8,128)(2,1)}) %all-gather.19.cloned.1.call-update) | async-done | bytes 6553616 | tf_op jit(solution)/shard_map/all_gather | solution.py:41
  133.9 74.5 %all-gather.17.cloned.1.call-done = bf16[1,160,8,5120]{3,2,0,1:T(8,128)(2,1)} async-done(((bf16[1,20,8,5120]{3,2,0,1:T(8,128)(2,1)}), bf16[1,160,8,5120]{3,2,0,1:T(8,128)(2,1)}) %all-gather.17.cloned.1.call-update) | async-done | bytes 13107216 | tf_op jit(solution)/shard_map/all_gather | solution.py:42
  208.4 15.1 %divide_bitcast_fusion.1 = f32[1,160,8,640]{3,2,1,0:T(8,128)S(1)} fusion(bf16[1,5120,640]{2,1,0:T(8,128)(2,1)} %all-gather.19.cloned.1.call-done, bf16[1,160,8,5120]{3,2,0,1:T(8,128)(2,1)} %all-gather.17.cloned.1.call-done, f32[640]{0:T(1024)S(1)} %dynamic_slice.21, f32[160,8]{1,0:T(8,128)S(1)} %copy.21), kind=kOutput, calls=%fused_computation.13 | convolution fusion | flops 8390246400 | bytes 22945280 | tf_op jit(solution)/shard_map/dot_general | solution.py:44
  223.6 106.1 %all-gather.15.cloned.1.call-done = bf16[1,5120,640]{2,1,0:T(8,128)(2,1)} async-done(((bf16[1,1280,640]{2,1,0:T(8,128)(2,1)}), bf16[1,5120,640]{2,1,0:T(8,128)(2,1)}) %all-gather.15.cloned.1.call-update) | async-done | bytes 6553616 | tf_op jit(solution)/shard_map/all_gather | solution.py:41
  329.7 74.4 %all-gather.13.cloned.1.call-done = bf16[1,160,8,5120]{3,2,0,1:T(8,128)(2,1)} async-done(((bf16[1,20,8,5120]{3,2,0,1:T(8,128)(2,1)}), bf16[1,160,8,5120]{3,2,0,1:T(8,128)(2,1)}) %all-gather.13.cloned.1.call-update) | async-done | bytes 13107216 | tf_op jit(solution)/shard_map/all_gather | solution.py:42
  404.0 16.0 %divide_bitcast_fusion.2 = f32[1,160,8,640]{3,2,1,0:T(8,128)} fusion(bf16[1,5120,640]{2,1,0:T(8,128)(2,1)} %all-gather.15.cloned.1.call-done, bf16[1,160,8,5120]{3,2,0,1:T(8,128)(2,1)} %all-gather.13.cloned.1.call-done, f32[640]{0:T(1024)S(1)} %dynamic_slice.19, f32[160,8]{1,0:T(8,128)S(1)} %copy.18), kind=kOutput, calls=%fused_computation.14 | convolution fusion | flops 8390246400 | bytes 22945280 | tf_op jit(solution)/shard_map/dot_general | solution.py:44
  420.0 105.1 %all-gather.23.cloned.1.call-done = bf16[1,5120,640]{2,1,0:T(8,128)(2,1)} async-done(((bf16[1,1280,640]{2,1,0:T(8,128)(2,1)}), bf16[1,5120,640]{2,1,0:T(8,128)(2,1)}) %all-gather.23.cloned.1.call-update) | async-done | bytes 6553616 | tf_op jit(solution)/shard_map/all_gather | solution.py:41
  525.1 74.4 %all-gather.21.cloned.1.call-done = bf16[1,160,8,5120]{3,2,0,1:T(8,128)(2,1)} async-done(((bf16[1,20,8,5120]{3,2,0,1:T(8,128)(2,1)}), bf16[1,160,8,5120]{3,2,0,1:T(8,128)(2,1)}) %all-gather.21.cloned.1.call-update) | async-done | bytes 13107216 | tf_op jit(solution)/shard_map/all_gather | solution.py:42
  599.5 15.3 %divide_bitcast_fusion = f32[1,160,8,640]{3,2,1,0:T(8,128)S(1)} fusion(bf16[1,5120,640]{2,1,0:T(8,128)(2,1)} %all-gather.23.cloned.1.call-done, bf16[1,160,8,5120]{3,2,0,1:T(8,128)(2,1)} %all-gather.21.cloned.1.call-done, f32[640]{0:T(1024)S(1)} %dynamic_slice.23, f32[160,8]{1,0:T(8,128)S(1)} %copy.24), kind=kOutput, calls=%fused_computation.12 | convolution fusion | flops 8390246400 | bytes 22945280 | tf_op jit(solution)/shard_map/dot_general | solution.py:44
  614.8 0.0 copy-done
  614.8 4.7 pad_maximum_fusion
  (10 shorter events, 0.0 us)
Async XLA Ops:
  6.5 127.4 %all-gather.19.cloned.1.call-start = ((), (), s32[]{:S(2)}) async-start(), calls=%async_computation.3 | async-start | bytes 8192000 | tf_op jit(solution)/shard_map/all_gather | solution.py:41
  11.4 197.0 %all-gather.17.cloned.1.call-start = ((), (), s32[]{:S(2)}) async-start(), calls=%async_computation.2 | async-start | bytes 14745600 | tf_op jit(solution)/shard_map/all_gather | solution.py:42
  16.2 2.5 copy-start.1
  16.2 2.5 copy-start.2
  16.2 3.6 copy-start.4
  16.2 3.6 copy-start.5
  16.2 3.9 copy-start.3
  16.2 313.4 %all-gather.15.cloned.1.call-start = ((), (), s32[]{:S(2)}) async-start(), calls=%async_computation.1 | async-start | bytes 8192000 | tf_op jit(solution)/shard_map/all_gather | solution.py:41
  17.0 387.1 %all-gather.13.cloned.1.call-start = ((), (), s32[]{:S(2)}) async-start(), calls=%async_computation | async-start | bytes 14745600 | tf_op jit(solution)/shard_map/all_gather | solution.py:42
  17.5 507.6 %all-gather.23.cloned.1.call-start = ((), (), s32[]{:S(2)}) async-start(), calls=%async_computation.5 | async-start | bytes 8192000 | tf_op jit(solution)/shard_map/all_gather | solution.py:41
  18.1 581.3 %all-gather.21.cloned.1.call-start = ((), (), s32[]{:S(2)}) async-start(), calls=%async_computation.4 | async-start | bytes 14745600 | tf_op jit(solution)/shard_map/all_gather | solution.py:42
  599.5 15.3 %copy-start = (f32[1,160,8,640]{3,2,1,0:T(8,128)S(1)}, f32[1,160,8,640]{3,2,1,0:T(8,128)}, u32[]{:S(2)}) copy-start(f32[1,160,8,640]{3,2,1,0:T(8,128)} %divide_bitcast_fusion.2) | copy-start | bytes 9830404
Sparse Core Ops, SparseCore 0:
  11.5 122.3 all-gather.18
  135.8 72.5 all-gather.16
  210.0 119.6 all-gather.14
  331.4 72.5 all-gather.12
  405.4 119.6 all-gather.22
  526.9 72.5 all-gather.20
where the time goes:
time: 626 us
  waiting for transfers between devices  549 us (88%)
  matrix products  46.4 us (7%)
  between operations  13.6 us (2%)
  local copies, waits for them, and re-layouts  10.8 us (2%)
    all_gather x3, waiting for transfers between devices, body(): whole_rows = lax.all_gather(integrals[block], 'row', axis=0, tiled=True)  324 us
    all_gather x3, waiting for transfers between devices, body(): piece = lax.all_gather(amplitudes[block], 'pair', axis=0, tiled=True)  223 us
    dot_general x3, matrix products, body(): product = jnp.dot(flat, whole_rows, preferred_element_type=jnp.float32)  46.4 us
  transfers between devices with their start and end apart: 6, of which 6 were waited for; matrix products, arithmetic and copies ran while one was open for 6% of the time, Pallas kernels for 0%

commit v1 on v0

--- a/solution.py
+++ b/solution.py
@@ -4,6 +4,19 @@
 from jax.sharding import PartitionSpec as P
 
 VIRG = 160
+
+
+def prepare_the_view(matrix):
+    amount_of = lax.axis_size("pair")
+    tmp = sorted(((w, (w + 1) % amount_of) for w in range(amount_of)))
+    tile_out = matrix
+    panels = [tile_out]
+    for t in [*range(1, amount_of)]:
+        tile_out = lax.ppermute(tile_out, "pair", tmp)
+        panels.insert(0, tile_out)
+    s_next = jnp.concatenate(panels, axis=0)
+    last = lax.axis_index("pair") + 1
+    return jnp.roll(s_next, last * matrix.shape[0], axis=0)
 
 
 def shift_table(occupied_irrep, virtual_order, block_irreps, occupied_energy, virtual_energy):
@@ -39,7 +52,7 @@
     results = []
     for block in range(block_count):
         whole_rows = lax.all_gather(integrals[block], "row", axis=0, tiled=True)
-        piece = lax.all_gather(amplitudes[block], "pair", axis=0, tiled=True)
+        piece = prepare_the_view(amplitudes[block])
         flat = piece.reshape(piece.shape[0] * piece.shape[1], piece.shape[2])
         product = jnp.dot(flat, whole_rows, preferred_element_type=jnp.float32)
         cycle_term = product.reshape(piece.shape[0], piece.shape[1], whole_rows.shape[1])

time: 626 us -> 474 us (0.76)
  waiting for transfers between devices: 549 us -> 339 us
  local copies, waits for them, and re-layouts: 10.8 us -> 53.8 us
  matrix products: 46.4 us -> 55.8 us
    ppermute x0 -> x21, waiting for transfers between devices: none -> 338 us  [prepare_the_view(): tile_out = lax.ppermute(tile_out, 'pair', tmp)]
    all_gather x3, waiting for transfers between devices: 324 us -> 0.02 us  [body(): whole_rows = lax.all_gather(integrals[block], 'row', axis=0, tiled=True)]
    all_gather x3 -> x0, waiting for transfers between devices: 223 us -> none  [body(): piece = lax.all_gather(amplitudes[block], 'pair', axis=0, tiled=True)]
    unnamed x13 -> x71, local copies, waits for them, and re-layouts: 4.74 us -> 41.5 us
    dot_general x3, matrix products: 46.4 us -> 55.8 us  [body(): product = jnp.dot(flat, whole_rows, preferred_element_type=jnp.float32)]
  transfers between devices with their start and end apart: 6 -> 24, of which waited for: 6 -> 21; matrix products, arithmetic and copies ran while one was open for 6% -> 18% of each run, Pallas kernels for 0% -> 0%
where the time goes in v1:
time: 474 us
  waiting for transfers between devices  339 us (72%)
  matrix products  55.8 us (12%)
  local copies, waits for them, and re-layouts  53.8 us (11%)
  between operations  13.3 us (3%)
  other arithmetic  8.71 us (2%)
    ppermute x21, waiting for transfers between devices, prepare_the_view(): tile_out = lax.ppermute(tile_out, 'pair', tmp)  338 us
    dot_general x3, matrix products, body(): product = jnp.dot(flat, whole_rows, preferred_element_type=jnp.float32)  55.8 us
    unnamed x71, local copies, waits for them, and re-layouts  41.5 us
  transfers between devices with their start and end apart: 24, of which 21 were waited for; matrix products, arithmetic and copies ran while one was open for 18% of the time, Pallas kernels for 0%

profile of v1, /device:TPU:0, one launch (start us, length us, event | category | flops | bytes accessed | tf_op | source)
XLA Modules:
  0.0 473.9 jit_solution(12392230026735193600)
XLA Ops:
  6.5 4.8 %fusion.30 = (bf16[1,1280,640]{2,1,0:T(8,128)(2,1)}, bf16[1,1280,640]{2,1,0:T(8,128)(2,1)}, bf16[1,1280,640]{2,1,0:T(8,128)(2,1)}) fusion(bf16[3,1280,640]{2,1,0:T(8,128)(2,1)} %param.10), kind=kLoop, calls=%fused_computation.61 | loop fusion | bytes 9830400 | tf_op jit(solution)/shard_map/slice | solution.py:54
  12.2 2.7 slice_bitcast_fusion.2
  15.4 2.6 collective-permute-start.7
  18.1 19.0 %collective-permute-done.14 = bf16[20,8,5120]{2,1,0:T(8,128)(2,1)S(1)} collective-permute-done((bf16[20,8,5120]{2,1,0:T(8,128)(2,1)S(1)}, bf16[20,8,5120]{2,1,0:T(8,128)(2,1)S(1)}, u32[]{:S(2)}, u32[]{:S(2)}) %collective-permute-start.14) | collective-permute-done | bytes 1638432 | tf_op jit(solution)/shard_map/ppermute | solution.py:15
  37.1 17.5 %collective-permute-done.7 = bf16[20,8,5120]{2,1,0:T(8,128)(2,1)S(1)} collective-permute-done((bf16[20,8,5120]{2,1,0:T(8,128)(2,1)S(1)}, bf16[20,8,5120]{2,1,0:T(8,128)(2,1)S(1)}, u32[]{:S(2)}, u32[]{:S(2)}) %collective-permute-start.7) | collective-permute-done | bytes 1638432 | tf_op jit(solution)/shard_map/ppermute | solution.py:15
  54.7 17.6 %collective-permute-done = bf16[20,8,5120]{2,1,0:T(8,128)(2,1)S(1)} collective-permute-done((bf16[20,8,5120]{2,1,0:T(8,128)(2,1)S(1)}, bf16[20,8,5120]{2,1,0:T(8,128)(2,1)S(1)}, u32[]{:S(2)}, u32[]{:S(2)}) %collective-permute-start) | collective-permute-done | bytes 1638432 | tf_op jit(solution)/shard_map/ppermute | solution.py:15
  72.2 17.6 %collective-permute-done.15 = bf16[20,8,5120]{2,1,0:T(8,128)(2,1)S(1)} collective-permute-done((bf16[20,8,5120]{2,1,0:T(8,128)(2,1)S(1)}, bf16[20,8,5120]{2,1,0:T(8,128)(2,1)S(1)}, u32[]{:S(2)}, u32[]{:S(2)}) %collective-permute-start.15) | collective-permute-done | bytes 1638432 | tf_op jit(solution)/shard_map/ppermute | solution.py:15
  89.8 17.5 %collective-permute-done.8 = bf16[20,8,5120]{2,1,0:T(8,128)(2,1)S(1)} collective-permute-done((bf16[20,8,5120]{2,1,0:T(8,128)(2,1)S(1)}, bf16[20,8,5120]{2,1,0:T(8,128)(2,1)S(1)}, u32[]{:S(2)}, u32[]{:S(2)}) %collective-permute-start.8) | collective-permute-done | bytes 1638432 | tf_op jit(solution)/shard_map/ppermute | solution.py:15
  107.4 17.5 %collective-permute-done.1 = bf16[20,8,5120]{2,1,0:T(8,128)(2,1)S(1)} collective-permute-done((bf16[20,8,5120]{2,1,0:T(8,128)(2,1)S(1)}, bf16[20,8,5120]{2,1,0:T(8,128)(2,1)S(1)}, u32[]{:S(2)}, u32[]{:S(2)}) %collective-permute-start.1) | collective-permute-done | bytes 1638432 | tf_op jit(solution)/shard_map/ppermute | solution.py:15
  126.1 16.4 %collective-permute-done.16 = bf16[20,8,5120]{2,1,0:T(8,128)(2,1)S(1)} collective-permute-done((bf16[20,8,5120]{2,1,0:T(8,128)(2,1)S(1)}, bf16[20,8,5120]{2,1,0:T(8,128)(2,1)S(1)}, u32[]{:S(2)}, u32[]{:S(2)}) %collective-permute-start.16) | collective-permute-done | bytes 1638432 | tf_op jit(solution)/shard_map/ppermute | solution.py:15
  142.5 17.5 %collective-permute-done.9 = bf16[20,8,5120]{2,1,0:T(8,128)(2,1)S(1)} collective-permute-done((bf16[20,8,5120]{2,1,0:T(8,128)(2,1)S(1)}, bf16[20,8,5120]{2,1,0:T(8,128)(2,1)S(1)}, u32[]{:S(2)}, u32[]{:S(2)}) %collective-permute-start.9) | collective-permute-done | bytes 1638432 | tf_op jit(solution)/shard_map/ppermute | solution.py:15
  160.0 17.5 %collective-permute-done.2 = bf16[20,8,5120]{2,1,0:T(8,128)(2,1)S(1)} collective-permute-done((bf16[20,8,5120]{2,1,0:T(8,128)(2,1)S(1)}, bf16[20,8,5120]{2,1,0:T(8,128)(2,1)S(1)}, u32[]{:S(2)}, u32[]{:S(2)}) %collective-permute-start.2) | collective-permute-done | bytes 1638432 | tf_op jit(solution)/shard_map/ppermute | solution.py:15
  177.6 17.5 %collective-permute-done.17 = bf16[20,8,5120]{2,1,0:T(8,128)(2,1)S(1)} collective-permute-done((bf16[20,8,5120]{2,1,0:T(8,128)(2,1)S(1)}, bf16[20,8,5120]{2,1,0:T(8,128)(2,1)S(1)}, u32[]{:S(2)}, u32[]{:S(2)}) %collective-permute-start.17) | collective-permute-done | bytes 1638432 | tf_op jit(solution)/shard_map/ppermute | solution.py:15
  195.1 17.6 %collective-permute-done.10 = bf16[20,8,5120]{2,1,0:T(8,128)(2,1)} collective-permute-done((bf16[20,8,5120]{2,1,0:T(8,128)(2,1)S(1)}, bf16[20,8,5120]{2,1,0:T(8,128)(2,1)}, u32[]{:S(2)}, u32[]{:S(2)}) %collective-permute-start.10) | collective-permute-done | bytes 1638432 | tf_op jit(solution)/shard_map/ppermute | solution.py:15
  212.8 17.6 %collective-permute-done.3 = bf16[20,8,5120]{2,1,0:T(8,128)(2,1)} collective-permute-done((bf16[20,8,5120]{2,1,0:T(8,128)(2,1)S(1)}, bf16[20,8,5120]{2,1,0:T(8,128)(2,1)}, u32[]{:S(2)}, u32[]{:S(2)}) %collective-permute-start.3) | collective-permute-done | bytes 1638432 | tf_op jit(solution)/shard_map/ppermute | solution.py:15
  230.4 17.5 %collective-permute-done.18 = bf16[20,8,5120]{2,1,0:T(8,128)(2,1)} collective-permute-done((bf16[20,8,5120]{2,1,0:T(8,128)(2,1)S(1)}, bf16[20,8,5120]{2,1,0:T(8,128)(2,1)}, u32[]{:S(2)}, u32[]{:S(2)}) %collective-permute-start.18) | collective-permute-done | bytes 1638432 | tf_op jit(solution)/shard_map/ppermute | solution.py:15
  248.0 17.5 %collective-permute-done.11 = bf16[20,8,5120]{2,1,0:T(8,128)(2,1)} collective-permute-done((bf16[20,8,5120]{2,1,0:T(8,128)(2,1)}, bf16[20,8,5120]{2,1,0:T(8,128)(2,1)}, u32[]{:S(2)}, u32[]{:S(2)}) %collective-permute-start.11) | collective-permute-done | bytes 1638432 | tf_op jit(solution)/shard_map/ppermute | solution.py:15
  265.5 17.6 %collective-permute-done.4 = bf16[20,8,5120]{2,1,0:T(8,128)(2,1)} collective-permute-done((bf16[20,8,5120]{2,1,0:T(8,128)(2,1)}, bf16[20,8,5120]{2,1,0:T(8,128)(2,1)}, u32[]{:S(2)}, u32[]{:S(2)}) %collective-permute-start.4) | collective-permute-done | bytes 1638432 | tf_op jit(solution)/shard_map/ppermute | solution.py:15
  283.0 17.6 %collective-permute-done.19 = bf16[20,8,5120]{2,1,0:T(8,128)(2,1)} collective-permute-done((bf16[20,8,5120]{2,1,0:T(8,128)(2,1)}, bf16[20,8,5120]{2,1,0:T(8,128)(2,1)}, u32[]{:S(2)}, u32[]{:S(2)}) %collective-permute-start.19) | collective-permute-done | bytes 1638432 | tf_op jit(solution)/shard_map/ppermute | solution.py:15
  304.4 13.7 %collective-permute-done.12 = bf16[20,8,5120]{2,1,0:T(8,128)(2,1)} collective-permute-done((bf16[20,8,5120]{2,1,0:T(8,128)(2,1)}, bf16[20,8,5120]{2,1,0:T(8,128)(2,1)}, u32[]{:S(2)}, u32[]{:S(2)}) %collective-permute-start.12) | collective-permute-done | bytes 1638432 | tf_op jit(solution)/shard_map/ppermute | solution.py:15
  318.1 17.6 %collective-permute-done.5 = bf16[20,8,5120]{2,1,0:T(8,128)(2,1)} collective-permute-done((bf16[20,8,5120]{2,1,0:T(8,128)(2,1)}, bf16[20,8,5120]{2,1,0:T(8,128)(2,1)}, u32[]{:S(2)}, u32[]{:S(2)}) %collective-permute-start.5) | collective-permute-done | bytes 1638432 | tf_op jit(solution)/shard_map/ppermute | solution.py:15
  335.7 17.6 %collective-permute-done.20 = bf16[20,8,5120]{2,1,0:T(8,128)(2,1)} collective-permute-done((bf16[20,8,5120]{2,1,0:T(8,128)(2,1)}, bf16[20,8,5120]{2,1,0:T(8,128)(2,1)}, u32[]{:S(2)}, u32[]{:S(2)}) %collective-permute-start.20) | collective-permute-done | bytes 1638432 | tf_op jit(solution)/shard_map/ppermute | solution.py:15
  353.2 2.7 constant_dynamic-update-slice_fusion.23
  356.0 2.7 constant_dynamic-update-slice_fusion.22
  358.6 2.7 constant_dynamic-update-slice_fusion.21
  361.4 1.3 constant_dynamic-update-slice_fusion.20
  362.7 1.4 constant_dynamic-update-slice_fusion.19
  364.1 1.3 constant_dynamic-update-slice_fusion.18
  365.4 1.3 constant_dynamic-update-slice_fusion.17
  366.7 4.0 collective-permute-done.13
  370.7 1.3 constant_dynamic-update-slice_fusion.15
  372.0 2.8 constant_dynamic-update-slice_fusion.14
  374.7 2.7 constant_dynamic-update-slice_fusion.13
  377.5 2.7 constant_dynamic-update-slice_fusion.12
  380.2 1.3 constant_dynamic-update-slice_fusion.11
  382.7 1.3 constant_dynamic-update-slice_fusion.9
  384.0 4.2 collective-permute-done.6
  389.5 2.9 constant_dynamic-update-slice_fusion.6
  392.4 2.7 constant_dynamic-update-slice_fusion.5
  395.1 2.7 constant_dynamic-update-slice_fusion.4
  397.8 1.3 constant_dynamic-update-slice_fusion.3
  399.1 1.3 constant_dynamic-update-slice_fusion.2
  400.4 1.3 constant_dynamic-update-slice_fusion.1
  401.7 2.3 constant_dynamic-update-slice_fusion
  404.0 17.3 %divide_bitcast_fusion.2 = f32[1,160,8,640]{3,2,1,0:T(8,128)S(1)} fusion(f32[640]{0:T(1024)S(1)} %dynamic_slice.22, f32[160,8]{1,0:T(8,128)S(1)} %copy.11, bf16[1,5120,640]{2,1,0:T(8,128)(2,1)} %all-gather.7.cloned.1.call-done, s32[]{:T(128)S(6)} %select_n.37, bf16[160,8,5120]{2,1,0:T(8,128)(2,1)} %get-tuple-element.6), kind=kOutput, calls=%fused_computation.20 | convolution fusion | flops 8396800000 | bytes 22945284 | tf_op jit(solution)/shard_map/dot_general | solution.py:57
  421.4 19.1 %divide_bitcast_fusion.1 = f32[1,160,8,640]{3,2,1,0:T(8,128)} fusion(f32[640]{0:T(1024)S(1)} %dynamic_slice.24, f32[160,8]{1,0:T(8,128)S(1)} %copy-done.16, bf16[1,5120,640]{2,1,0:T(8,128)(2,1)} %all-gather.9.cloned.1.call-done, s32[]{:T(128)S(6)} %select_n.37, bf16[160,8,5120]{2,1,0:T(8,128)(2,1)} %get-tuple-element.8), kind=kOutput, calls=%fused_computation.19 | convolution fusion | flops 8396800000 | bytes 22945284 | tf_op jit(solution)/shard_map/dot_general | solution.py:57
  440.6 19.3 %divide_bitcast_fusion = f32[1,160,8,640]{3,2,1,0:T(8,128)} fusion(f32[640]{0:T(1024)S(1)} %dynamic_slice.26, f32[160,8]{1,0:T(8,128)S(1)} %copy-done.17, bf16[1,5120,640]{2,1,0:T(8,128)(2,1)} %all-gather.11.cloned.1.call-done, s32[]{:T(128)S(6)} %select_n.37, bf16[160,8,5120]{2,1,0:T(8,128)(2,1)} %get-tuple-element.7), kind=kOutput, calls=%fused_computation.18 | convolution fusion | flops 8396800000 | bytes 22945284 | tf_op jit(solution)/shard_map/dot_general | solution.py:57
  459.9 7.4 %pad_maximum_fusion = f32[3,160,8,640]{3,2,1,0:T(8,128)} fusion(f32[1,160,8,640]{3,2,1,0:T(8,128)} %divide_bitcast_fusion, f32[1,160,8,640]{3,2,1,0:T(8,128)} %divide_bitcast_fusion.1, f32[1,160,8,640]{3,2,1,0:T(8,128)S(1)} %divide_bitcast_fusion.2), kind=kLoop, calls=%fused_computation.12 | loop fusion | flops 4915200 | bytes 19660800 | tf_op jit(solution)/shard_map/stack | solution.py:65
  (104 shorter events, 9.0 us)
Async XLA Ops:
  6.5 397.5 %all-gather.7.cloned.1.call-start = ((), (), s32[]{:S(2)}) async-start(), calls=%async_computation | async-start | bytes 8192000 | tf_op jit(solution)/shard_map/all_gather | solution.py:54
  11.3 289.2 %copy-start.18 = (f32[1280]{0:T(1024)S(1)}, f32[1280]{0:T(1024)}, u32[]{:S(2)}) copy-start(f32[1280]{0:T(1024)} %param.15) | copy-start | bytes 15364
  11.3 289.2 %copy-start.19 = (s32[1280]{0:T(1024)S(1)}, s32[1280]{0:T(1024)}, u32[]{:S(2)}) copy-start(s32[1280]{0:T(1024)} %param.12) | copy-start | bytes 15364
  11.3 290.3 %copy-start.21 = (s32[32]{0:T(128)S(1)}, s32[32]{0:T(128)}, u32[]{:S(2)}) copy-start(s32[32]{0:T(128)} %param.11) | copy-start | bytes 388
  11.4 290.3 %copy-start.22 = (s32[3]{0:T(128)S(1)}, s32[3]{0:T(128)}, u32[]{:S(2)}) copy-start(s32[3]{0:T(128)} %param.13) | copy-start | bytes 40
  11.4 290.5 %copy-start.20 = (f32[32]{0:T(128)S(1)}, f32[32]{0:T(128)}, u32[]{:S(2)}) copy-start(f32[32]{0:T(128)} %param.14) | copy-start | bytes 388
  11.4 410.0 %all-gather.9.cloned.1.call-start = ((), (), s32[]{:S(2)}) async-start(), calls=%async_computation.1 | async-start | bytes 8192000 | tf_op jit(solution)/shard_map/all_gather | solution.py:54
  12.1 428.4 %all-gather.11.cloned.1.call-start = ((), (), s32[]{:S(2)}) async-start(), calls=%async_computation.2 | async-start | bytes 8192000 | tf_op jit(solution)/shard_map/all_gather | solution.py:54
  14.9 22.2 %collective-permute-start.14 = (bf16[20,8,5120]{2,1,0:T(8,128)(2,1)S(1)}, bf16[20,8,5120]{2,1,0:T(8,128)(2,1)S(1)}, u32[]{:S(2)}, u32[]{:S(2)}) collective-permute-start(bf16[20,8,5120]{2,1,0:T(8,128)(2,1)S(1)} %get-tuple-element.10), channel_id=1, source_target_pairs={{0,4},{4,8},{8,12},{12,16},{16,20},{20,24},{24,28},{28,0},{1,5},{5... | collective-permute-start | bytes 4915208 | tf_op jit(solution)/shard_map/ppermute | solution.py:15
  15.4 39.2 %collective-permute-start.7 = (bf16[20,8,5120]{2,1,0:T(8,128)(2,1)S(1)}, bf16[20,8,5120]{2,1,0:T(8,128)(2,1)S(1)}, u32[]{:S(2)}, u32[]{:S(2)}) collective-permute-start(bf16[20,8,5120]{2,1,0:T(8,128)(2,1)S(1)} %get-tuple-element.11), channel_id=1, source_target_pairs={{0,4},{4,8},{8,12},{12,16},{16,20},{20,24},{24,28},{28,0},{1,5},{5... | collective-permute-start | bytes 4915208 | tf_op jit(solution)/shard_map/ppermute | solution.py:15
  18.0 54.2 %collective-permute-start = (bf16[20,8,5120]{2,1,0:T(8,128)(2,1)S(1)}, bf16[20,8,5120]{2,1,0:T(8,128)(2,1)S(1)}, u32[]{:S(2)}, u32[]{:S(2)}) collective-permute-start(bf16[20,8,5120]{2,1,0:T(8,128)(2,1)S(1)} %get-tuple-element.9), channel_id=1, source_target_pairs={{0,4},{4,8},{8,12},{12,16},{16,20},{20,24},{24,28},{28,0},{1,5},{5... | collective-permute-start | bytes 4915208 | tf_op jit(solution)/shard_map/ppermute | solution.py:15
  37.1 140.4 %copy-start.2 = (bf16[20,8,5120]{2,1,0:T(8,128)(2,1)}, bf16[20,8,5120]{2,1,0:T(8,128)(2,1)S(1)}, u32[]{:S(2)}) copy-start(bf16[20,8,5120]{2,1,0:T(8,128)(2,1)S(1)} %collective-permute-done.14) | copy-start | bytes 4915204
  37.1 52.7 %collective-permute-start.15 = (bf16[20,8,5120]{2,1,0:T(8,128)(2,1)S(1)}, bf16[20,8,5120]{2,1,0:T(8,128)(2,1)S(1)}, u32[]{:S(2)}, u32[]{:S(2)}) collective-permute-start(bf16[20,8,5120]{2,1,0:T(8,128)(2,1)S(1)} %collective-permute-done.14), channel_id=1, source_target_pairs={{0,4},{4,8},{8,12},{12,16},{16,20},{20,24},{24,28},{28,0},{1,5},{5... | collective-permute-start | bytes 4915208 | tf_op jit(solution)/shard_map/ppermute | solution.py:15
  54.7 52.7 %collective-permute-start.8 = (bf16[20,8,5120]{2,1,0:T(8,128)(2,1)S(1)}, bf16[20,8,5120]{2,1,0:T(8,128)(2,1)S(1)}, u32[]{:S(2)}, u32[]{:S(2)}) collective-permute-start(bf16[20,8,5120]{2,1,0:T(8,128)(2,1)S(1)} %collective-permute-done.7), channel_id=1, source_target_pairs={{0,4},{4,8},{8,12},{12,16},{16,20},{20,24},{24,28},{28,0},{1,5},{5... | collective-permute-start | bytes 4915208 | tf_op jit(solution)/shard_map/ppermute | solution.py:15
  72.2 52.7 %collective-permute-start.1 = (bf16[20,8,5120]{2,1,0:T(8,128)(2,1)S(1)}, bf16[20,8,5120]{2,1,0:T(8,128)(2,1)S(1)}, u32[]{:S(2)}, u32[]{:S(2)}) collective-permute-start(bf16[20,8,5120]{2,1,0:T(8,128)(2,1)S(1)} %collective-permute-done), channel_id=1, source_target_pairs={{0,4},{4,8},{8,12},{12,16},{16,20},{20,24},{24,28},{28,0},{1,5},{5... | collective-permute-start | bytes 4915208 | tf_op jit(solution)/shard_map/ppermute | solution.py:15
  89.8 140.5 %copy-start.8 = (bf16[20,8,5120]{2,1,0:T(8,128)(2,1)}, bf16[20,8,5120]{2,1,0:T(8,128)(2,1)S(1)}, u32[]{:S(2)}) copy-start(bf16[20,8,5120]{2,1,0:T(8,128)(2,1)S(1)} %collective-permute-done.15) | copy-start | bytes 4915204
  89.8 52.7 %collective-permute-start.16 = (bf16[20,8,5120]{2,1,0:T(8,128)(2,1)S(1)}, bf16[20,8,5120]{2,1,0:T(8,128)(2,1)S(1)}, u32[]{:S(2)}, u32[]{:S(2)}) collective-permute-start(bf16[20,8,5120]{2,1,0:T(8,128)(2,1)S(1)} %collective-permute-done.15), channel_id=1, source_target_pairs={{0,4},{4,8},{8,12},{12,16},{16,20},{20,24},{24,28},{28,0},{1,5},{5... | collective-permute-start | bytes 4915208 | tf_op jit(solution)/shard_map/ppermute | solution.py:15
  107.3 70.2 %copy-start.4 = (bf16[20,8,5120]{2,1,0:T(8,128)(2,1)}, bf16[20,8,5120]{2,1,0:T(8,128)(2,1)S(1)}, u32[]{:S(2)}) copy-start(bf16[20,8,5120]{2,1,0:T(8,128)(2,1)S(1)} %collective-permute-done.8) | copy-start | bytes 4915204
  107.4 52.7 %collective-permute-start.9 = (bf16[20,8,5120]{2,1,0:T(8,128)(2,1)S(1)}, bf16[20,8,5120]{2,1,0:T(8,128)(2,1)S(1)}, u32[]{:S(2)}, u32[]{:S(2)}) collective-permute-start(bf16[20,8,5120]{2,1,0:T(8,128)(2,1)S(1)} %collective-permute-done.8), channel_id=1, source_target_pairs={{0,4},{4,8},{8,12},{12,16},{16,20},{20,24},{24,28},{28,0},{1,5},{5... | collective-permute-start | bytes 4915208 | tf_op jit(solution)/shard_map/ppermute | solution.py:15
  126.1 51.5 %collective-permute-start.2 = (bf16[20,8,5120]{2,1,0:T(8,128)(2,1)S(1)}, bf16[20,8,5120]{2,1,0:T(8,128)(2,1)S(1)}, u32[]{:S(2)}, u32[]{:S(2)}) collective-permute-start(bf16[20,8,5120]{2,1,0:T(8,128)(2,1)S(1)} %collective-permute-done.1), channel_id=1, source_target_pairs={{0,4},{4,8},{8,12},{12,16},{16,20},{20,24},{24,28},{28,0},{1,5},{5... | collective-permute-start | bytes 4915208 | tf_op jit(solution)/shard_map/ppermute | solution.py:15
  142.5 105.4 %copy-start.12 = (bf16[20,8,5120]{2,1,0:T(8,128)(2,1)}, bf16[20,8,5120]{2,1,0:T(8,128)(2,1)S(1)}, u32[]{:S(2)}) copy-start(bf16[20,8,5120]{2,1,0:T(8,128)(2,1)S(1)} %collective-permute-done.16) | copy-start | bytes 4915204
  142.5 52.7 %collective-permute-start.17 = (bf16[20,8,5120]{2,1,0:T(8,128)(2,1)S(1)}, bf16[20,8,5120]{2,1,0:T(8,128)(2,1)S(1)}, u32[]{:S(2)}, u32[]{:S(2)}) collective-permute-start(bf16[20,8,5120]{2,1,0:T(8,128)(2,1)S(1)} %collective-permute-done.16), channel_id=1, source_target_pairs={{0,4},{4,8},{8,12},{12,16},{16,20},{20,24},{24,28},{28,0},{1,5},{5... | collective-permute-start | bytes 4915208 | tf_op jit(solution)/shard_map/ppermute | solution.py:15
  160.0 70.3 %copy-start.10 = (bf16[20,8,5120]{2,1,0:T(8,128)(2,1)}, bf16[20,8,5120]{2,1,0:T(8,128)(2,1)S(1)}, u32[]{:S(2)}) copy-start(bf16[20,8,5120]{2,1,0:T(8,128)(2,1)S(1)} %collective-permute-done.9) | copy-start | bytes 4915204
  160.0 52.8 %collective-permute-start.10 = (bf16[20,8,5120]{2,1,0:T(8,128)(2,1)S(1)}, bf16[20,8,5120]{2,1,0:T(8,128)(2,1)}, u32[]{:S(2)}, u32[]{:S(2)}) collective-permute-start(bf16[20,8,5120]{2,1,0:T(8,128)(2,1)S(1)} %collective-permute-done.9), channel_id=1, source_target_pairs={{0,4},{4,8},{8,12},{12,16},{16,20},{20,24},{24,28},{28,0},{1,5},{5... | collective-permute-start | bytes 4915208 | tf_op jit(solution)/shard_map/ppermute | solution.py:15
  177.6 17.6 %copy-start.6 = (bf16[20,8,5120]{2,1,0:T(8,128)(2,1)}, bf16[20,8,5120]{2,1,0:T(8,128)(2,1)S(1)}, u32[]{:S(2)}) copy-start(bf16[20,8,5120]{2,1,0:T(8,128)(2,1)S(1)} %collective-permute-done.2) | copy-start | bytes 4915204
  177.6 52.8 %collective-permute-start.3 = (bf16[20,8,5120]{2,1,0:T(8,128)(2,1)S(1)}, bf16[20,8,5120]{2,1,0:T(8,128)(2,1)}, u32[]{:S(2)}, u32[]{:S(2)}) collective-permute-start(bf16[20,8,5120]{2,1,0:T(8,128)(2,1)S(1)} %collective-permute-done.2), channel_id=1, source_target_pairs={{0,4},{4,8},{8,12},{12,16},{16,20},{20,24},{24,28},{28,0},{1,5},{5... | collective-permute-start | bytes 4915208 | tf_op jit(solution)/shard_map/ppermute | solution.py:15
  195.1 52.8 %copy-start.14 = (bf16[20,8,5120]{2,1,0:T(8,128)(2,1)}, bf16[20,8,5120]{2,1,0:T(8,128)(2,1)S(1)}, u32[]{:S(2)}) copy-start(bf16[20,8,5120]{2,1,0:T(8,128)(2,1)S(1)} %collective-permute-done.17) | copy-start | bytes 4915204
  195.1 52.8 %collective-permute-start.18 = (bf16[20,8,5120]{2,1,0:T(8,128)(2,1)S(1)}, bf16[20,8,5120]{2,1,0:T(8,128)(2,1)}, u32[]{:S(2)}, u32[]{:S(2)}) collective-permute-start(bf16[20,8,5120]{2,1,0:T(8,128)(2,1)S(1)} %collective-permute-done.17), channel_id=1, source_target_pairs={{0,4},{4,8},{8,12},{12,16},{16,20},{20,24},{24,28},{28,0},{1,5},{5... | collective-permute-start | bytes 4915208 | tf_op jit(solution)/shard_map/ppermute | solution.py:15
  212.8 52.7 %collective-permute-start.11 = (bf16[20,8,5120]{2,1,0:T(8,128)(2,1)}, bf16[20,8,5120]{2,1,0:T(8,128)(2,1)}, u32[]{:S(2)}, u32[]{:S(2)}) collective-permute-start(bf16[20,8,5120]{2,1,0:T(8,128)(2,1)} %collective-permute-done.10), channel_id=1, source_target_pairs={{0,4},{4,8},{8,12},{12,16},{16,20},{20,24},{24,28},{28,0},{1,5},{5... | collective-permute-start | bytes 4915208 | tf_op jit(solution)/shard_map/ppermute | solution.py:15
  230.3 52.7 %collective-permute-start.4 = (bf16[20,8,5120]{2,1,0:T(8,128)(2,1)}, bf16[20,8,5120]{2,1,0:T(8,128)(2,1)}, u32[]{:S(2)}, u32[]{:S(2)}) collective-permute-start(bf16[20,8,5120]{2,1,0:T(8,128)(2,1)} %collective-permute-done.3), channel_id=1, source_target_pairs={{0,4},{4,8},{8,12},{12,16},{16,20},{20,24},{24,28},{28,0},{1,5},{5... | collective-permute-start | bytes 4915208 | tf_op jit(solution)/shard_map/ppermute | solution.py:15
  247.9 52.7 %collective-permute-start.19 = (bf16[20,8,5120]{2,1,0:T(8,128)(2,1)}, bf16[20,8,5120]{2,1,0:T(8,128)(2,1)}, u32[]{:S(2)}, u32[]{:S(2)}) collective-permute-start(bf16[20,8,5120]{2,1,0:T(8,128)(2,1)} %collective-permute-done.18), channel_id=1, source_target_pairs={{0,4},{4,8},{8,12},{12,16},{16,20},{20,24},{24,28},{28,0},{1,5},{5... | collective-permute-start | bytes 4915208 | tf_op jit(solution)/shard_map/ppermute | solution.py:15
  265.5 52.7 %collective-permute-start.12 = (bf16[20,8,5120]{2,1,0:T(8,128)(2,1)}, bf16[20,8,5120]{2,1,0:T(8,128)(2,1)}, u32[]{:S(2)}, u32[]{:S(2)}) collective-permute-start(bf16[20,8,5120]{2,1,0:T(8,128)(2,1)} %collective-permute-done.11), channel_id=1, source_target_pairs={{0,4},{4,8},{8,12},{12,16},{16,20},{20,24},{24,28},{28,0},{1,5},{5... | collective-permute-start | bytes 4915208 | tf_op jit(solution)/shard_map/ppermute | solution.py:15
  283.0 52.7 %collective-permute-start.5 = (bf16[20,8,5120]{2,1,0:T(8,128)(2,1)}, bf16[20,8,5120]{2,1,0:T(8,128)(2,1)}, u32[]{:S(2)}, u32[]{:S(2)}) collective-permute-start(bf16[20,8,5120]{2,1,0:T(8,128)(2,1)} %collective-permute-done.4), channel_id=1, source_target_pairs={{0,4},{4,8},{8,12},{12,16},{16,20},{20,24},{24,28},{28,0},{1,5},{5... | collective-permute-start | bytes 4915208 | tf_op jit(solution)/shard_map/ppermute | solution.py:15
  300.6 52.7 %collective-permute-start.20 = (bf16[20,8,5120]{2,1,0:T(8,128)(2,1)}, bf16[20,8,5120]{2,1,0:T(8,128)(2,1)}, u32[]{:S(2)}, u32[]{:S(2)}) collective-permute-start(bf16[20,8,5120]{2,1,0:T(8,128)(2,1)} %collective-permute-done.19), channel_id=1, source_target_pairs={{0,4},{4,8},{8,12},{12,16},{16,20},{20,24},{24,28},{28,0},{1,5},{5... | collective-permute-start | bytes 4915208 | tf_op jit(solution)/shard_map/ppermute | solution.py:15
  304.4 57.0 %copy-start.15 = (bf16[20,8,5120]{2,1,0:T(8,128)(2,1)S(1)}, bf16[20,8,5120]{2,1,0:T(8,128)(2,1)}, u32[]{:S(2)}) copy-start(bf16[20,8,5120]{2,1,0:T(8,128)(2,1)} %copy-done.14) | copy-start | bytes 4915204
  304.4 58.3 %copy-start.13 = (bf16[20,8,5120]{2,1,0:T(8,128)(2,1)S(1)}, bf16[20,8,5120]{2,1,0:T(8,128)(2,1)}, u32[]{:S(2)}) copy-start(bf16[20,8,5120]{2,1,0:T(8,128)(2,1)} %copy-done.12) | copy-start | bytes 4915204
  304.4 59.7 %copy-start.9 = (bf16[20,8,5120]{2,1,0:T(8,128)(2,1)S(1)}, bf16[20,8,5120]{2,1,0:T(8,128)(2,1)}, u32[]{:S(2)}) copy-start(bf16[20,8,5120]{2,1,0:T(8,128)(2,1)} %copy-done.8) | copy-start | bytes 4915204
  304.4 61.0 %copy-start.3 = (bf16[20,8,5120]{2,1,0:T(8,128)(2,1)S(1)}, bf16[20,8,5120]{2,1,0:T(8,128)(2,1)}, u32[]{:S(2)}) copy-start(bf16[20,8,5120]{2,1,0:T(8,128)(2,1)} %copy-done.2) | copy-start | bytes 4915204
  318.1 52.6 %collective-permute-start.13 = (bf16[20,8,5120]{2,1,0:T(8,128)(2,1)}, bf16[20,8,5120]{2,1,0:T(8,128)(2,1)S(1)}, u32[]{:S(2)}, u32[]{:S(2)}) collective-permute-start(bf16[20,8,5120]{2,1,0:T(8,128)(2,1)} %collective-permute-done.12), channel_id=1, source_target_pairs={{0,4},{4,8},{8,12},{12,16},{16,20},{20,24},{24,28},{28,0},{1,5},{5... | collective-permute-start | bytes 4915208 | tf_op jit(solution)/shard_map/ppermute | solution.py:15
  335.7 52.6 %collective-permute-start.6 = (bf16[20,8,5120]{2,1,0:T(8,128)(2,1)}, bf16[20,8,5120]{2,1,0:T(8,128)(2,1)S(1)}, u32[]{:S(2)}, u32[]{:S(2)}) collective-permute-start(bf16[20,8,5120]{2,1,0:T(8,128)(2,1)} %collective-permute-done.5), channel_id=1, source_target_pairs={{0,4},{4,8},{8,12},{12,16},{16,20},{20,24},{24,28},{28,0},{1,5},{5... | collective-permute-start | bytes 4915208 | tf_op jit(solution)/shard_map/ppermute | solution.py:15
  364.1 16.1 %copy-start.11 = (bf16[20,8,5120]{2,1,0:T(8,128)(2,1)S(1)}, bf16[20,8,5120]{2,1,0:T(8,128)(2,1)}, u32[]{:S(2)}) copy-start(bf16[20,8,5120]{2,1,0:T(8,128)(2,1)} %copy-done.10) | copy-start | bytes 4915204
  365.4 16.0 %copy-start.5 = (bf16[20,8,5120]{2,1,0:T(8,128)(2,1)S(1)}, bf16[20,8,5120]{2,1,0:T(8,128)(2,1)}, u32[]{:S(2)}) copy-start(bf16[20,8,5120]{2,1,0:T(8,128)(2,1)} %copy-done.4) | copy-start | bytes 4915204
  381.4 16.4 %copy-start.7 = (bf16[20,8,5120]{2,1,0:T(8,128)(2,1)S(1)}, bf16[20,8,5120]{2,1,0:T(8,128)(2,1)}, u32[]{:S(2)}) copy-start(bf16[20,8,5120]{2,1,0:T(8,128)(2,1)} %copy-done.6) | copy-start | bytes 4915204
  382.7 16.4 %copy-start.1 = (bf16[20,8,5120]{2,1,0:T(8,128)(2,1)S(1)}, bf16[20,8,5120]{2,1,0:T(8,128)(2,1)}, u32[]{:S(2)}) copy-start(bf16[20,8,5120]{2,1,0:T(8,128)(2,1)} %copy-done) | copy-start | bytes 4915204
  389.5 12.2 %slice-start = ((s8[4915200]{0:T(1024)(128)(4,1)}), s8[4194304]{0:T(1024)(128)(4,1)S(1)}, s32[]{:S(2)}) async-start(s8[4915200]{0:T(1024)(128)(4,1)} %bitcast.42), calls=%async_computation.3 | async-start | bytes 8388608
  397.8 3.9 slice-start.1
  404.0 17.4 %copy-start.16 = (f32[160,8]{1,0:T(8,128)S(1)}, f32[160,8]{1,0:T(8,128)}, u32[]{:S(2)}) copy-start(f32[160,8]{1,0:T(8,128)} %copy.13) | copy-start | bytes 15364
  421.4 19.2 %copy-start.17 = (f32[160,8]{1,0:T(8,128)S(1)}, f32[160,8]{1,0:T(8,128)}, u32[]{:S(2)}) copy-start(f32[160,8]{1,0:T(8,128)} %copy.15) | copy-start | bytes 15364
  (1 other events, 1.2 us)
Sparse Core Ops, SparseCore 0:
  11.5 122.3 all-gather.6
  135.5 117.8 all-gather.8
  254.9 117.8 all-gather.10
